TPU v7x, 32 devices: a whole 2x2x4 slice. The times are simulated.
32 devices in a mesh: pair: 8 (over z, y), aux: 4 (over x, core).
Axes of the slice: x: 2, y: 2, z: 4, core: 2. Of those that a mesh axis runs over, the one named last changes fastest.
Arguments:
- pair_factors: bfloat16 [16384, 16384], P('pair', 'aux'), may hold values from -0.077339804 to 0.077339804
- pair_weights: float32 [16384], P('pair'), may hold values from 0.08 to 0.8
- probes: float32 [16384, 64], P('aux'), may hold values from -12 to 12
Outputs:
- last_vectors: float32 [16384, 64], P('aux', 'pair')
- moments: float32 [9], replicated
- energy: float32 [1], replicated
All inputs are finite; a program needn't handle non-finite values.
Results may differ from a plain program's by a relative error of at most 0.019.
Values may be sent and summed in bfloat16 or wider, within the bound.
No kernel may reach another device: no remote copies, remote signals or barrier semaphores. Data moves between devices by JAX's collectives and lax.ppermute only.
A program may use at most 64 MiB of HBM per device.

v0:
```python
import jax
import jax.numpy as jnp
import numpy as np
from jax import lax
from jax.sharding import PartitionSpec as P

ITERS = 8
spread = 5.0


def cheb_coefficients(order_count):
    node_count = 64
    angles = (np.arange(node_count) + 0.5) * np.pi / node_count
    samples = np.log(1.0 + spread * (np.cos(angles) + 1.0) / 2.0)
    values = [
        2.0 / node_count * np.sum(samples * np.cos(degree * angles))
        for degree in range(order_count)
    ]
    values[0] = values[0] / 2.0
    return np.array(values)


def per_device(pair_factors, pair_weights, probes):
    probe_total = probes.shape[1]
    divisor = probe_total * probes.shape[0] * lax.axis_size("aux")
    share = probe_total // lax.axis_size("pair")
    start = lax.axis_index("pair") * share
    own_probes = lax.dynamic_slice_in_dim(probes, start, share, 1)
    partials = [jnp.sum(own_probes * own_probes)]
    previous = probes
    current = probes
    for degree in range(ITERS):
        rows = jnp.dot(
            pair_factors, current.astype(jnp.bfloat16), preferred_element_type=jnp.float32
        )
        rows = lax.psum(rows, "aux")
        scaled = (pair_weights[:, None] * rows).astype(jnp.bfloat16)
        image = lax.psum(
            lax.dot_general(
                pair_factors, scaled, (((0,), (0,)), ((), ())), preferred_element_type=jnp.float32
            ),
            "pair",
        )
        mapped = 2.0 / spread * image - current
        following = mapped if degree == 0 else 2.0 * mapped - previous
        previous, current = (current, following)
        own_share = lax.dynamic_slice_in_dim(current, start, share, 1)
        partials.append(jnp.sum(own_probes * own_share))
    own_share = lax.dynamic_slice_in_dim(current, start, share, 1)
    totals = lax.psum(jnp.stack(partials), ("pair", "aux"))
    moments = totals / divisor
    coefficients = jnp.asarray(cheb_coefficients(ITERS + 1)).astype(moments.dtype)
    energy = jnp.sum(coefficients * moments).reshape(1)
    return (own_share, moments, energy)


def solution(mesh):
    placed = (P("pair", "aux"), P("pair"), P("aux", None))
    return jax.shard_map(
        per_device,
        mesh=mesh,
        in_specs=placed,
        out_specs=(P("aux", "pair"), P(), P()),
        check_vma=False,
    )
```

profile of v0, /device:TPU:0, one launch (start us, length us, event | category | flops | bytes accessed | tf_op | source)
XLA Modules:
  0.0 1159.6 jit_solution(14180925838934480082)
XLA Ops:
  7.2 11.6 fusion.7
  18.8 39.1 %all-reduce.17.cloned.1.call-done = f32[2048,64]{1,0:T(8,128)} async-done(((f32[2048,64]{1,0:T(8,128)}), f32[2048,64]{1,0:T(8,128)}) %all-reduce.17.cloned.1.call-update) | async-done | bytes 524304 | tf_op jit(solution)/shard_map/psum | solution.py:36
  58.0 10.3 convolution_bitcast_fusion.7
  68.3 78.9 %all-reduce.19.cloned.1.call-done = f32[4096,64]{0,1:T(8,128)} async-done(((f32[4096,64]{0,1:T(8,128)}), f32[4096,64]{0,1:T(8,128)}) %all-reduce.19.cloned.1.call-update) | async-done | bytes 1048592 | tf_op jit(solution)/shard_map/psum | solution.py:38
  147.3 1.3 multiply_subtract_fusion.6
  148.6 9.2 convolution_bitcast_fusion.14
  157.8 0.6 all-reduce.23.cloned.1.call-start
  158.4 35.5 %all-reduce.21.cloned.1.call-done = f32[2048,64]{1,0:T(8,128)} async-done(((f32[2048,64]{1,0:T(8,128)}), f32[2048,64]{1,0:T(8,128)}) %all-reduce.21.cloned.1.call-update) | async-done | bytes 524304 | tf_op jit(solution)/shard_map/psum | solution.py:36
  193.8 10.3 convolution_bitcast_fusion.6
  204.2 79.0 %all-reduce.23.cloned.1.call-done = f32[4096,64]{0,1:T(8,128)} async-done(((f32[4096,64]{0,1:T(8,128)}), f32[4096,64]{0,1:T(8,128)}) %all-reduce.23.cloned.1.call-update) | async-done | bytes 1048592 | tf_op jit(solution)/shard_map/psum | solution.py:38
  283.2 1.4 multiply_subtract_fusion.5
  284.6 9.2 convolution_bitcast_fusion.13
  293.8 36.0 %all-reduce.25.cloned.1.call-done = f32[2048,64]{1,0:T(8,128)} async-done(((f32[2048,64]{1,0:T(8,128)}), f32[2048,64]{1,0:T(8,128)}) %all-reduce.25.cloned.1.call-update) | async-done | bytes 524304 | tf_op jit(solution)/shard_map/psum | solution.py:36
  329.8 10.3 convolution_bitcast_fusion.5
  340.2 79.0 %all-reduce.27.cloned.1.call-done = f32[4096,64]{0,1:T(8,128)} async-done(((f32[4096,64]{0,1:T(8,128)}), f32[4096,64]{0,1:T(8,128)}) %all-reduce.27.cloned.1.call-update) | async-done | bytes 1048592 | tf_op jit(solution)/shard_map/psum | solution.py:38
  419.2 1.4 multiply_subtract_fusion.4
  420.6 9.2 convolution_bitcast_fusion.12
  430.0 35.8 %all-reduce.29.cloned.1.call-done = f32[2048,64]{1,0:T(8,128)} async-done(((f32[2048,64]{1,0:T(8,128)}), f32[2048,64]{1,0:T(8,128)}) %all-reduce.29.cloned.1.call-update) | async-done | bytes 524304 | tf_op jit(solution)/shard_map/psum | solution.py:36
  465.8 10.3 convolution_bitcast_fusion.4
  476.2 79.0 %all-reduce.31.cloned.1.call-done = f32[4096,64]{0,1:T(8,128)} async-done(((f32[4096,64]{0,1:T(8,128)}), f32[4096,64]{0,1:T(8,128)}) %all-reduce.31.cloned.1.call-update) | async-done | bytes 1048592 | tf_op jit(solution)/shard_map/psum | solution.py:38
  555.2 1.4 multiply_subtract_fusion.3
  556.6 1.0 copy-done
  557.5 9.1 convolution_bitcast_fusion.11
  566.7 36.0 %all-reduce.33.cloned.1.call-done = f32[2048,64]{1,0:T(8,128)} async-done(((f32[2048,64]{1,0:T(8,128)}), f32[2048,64]{1,0:T(8,128)}) %all-reduce.33.cloned.1.call-update) | async-done | bytes 524304 | tf_op jit(solution)/shard_map/psum | solution.py:36
  602.7 10.2 convolution_bitcast_fusion.3
  613.0 78.9 %all-reduce.35.cloned.1.call-done = f32[4096,64]{0,1:T(8,128)} async-done(((f32[4096,64]{0,1:T(8,128)}), f32[4096,64]{0,1:T(8,128)}) %all-reduce.35.cloned.1.call-update) | async-done | bytes 1048592 | tf_op jit(solution)/shard_map/psum | solution.py:38
  691.9 1.7 multiply_subtract_fusion.2
  693.6 1.0 copy-done.1
  694.7 9.1 convolution_bitcast_fusion.10
  704.0 35.8 %all-reduce.37.cloned.1.call-done = f32[2048,64]{1,0:T(8,128)} async-done(((f32[2048,64]{1,0:T(8,128)}), f32[2048,64]{1,0:T(8,128)}) %all-reduce.37.cloned.1.call-update) | async-done | bytes 524304 | tf_op jit(solution)/shard_map/psum | solution.py:36
  739.8 10.2 convolution_bitcast_fusion.2
  750.2 78.8 %all-reduce.39.cloned.1.call-done = f32[4096,64]{0,1:T(8,128)} async-done(((f32[4096,64]{0,1:T(8,128)}), f32[4096,64]{0,1:T(8,128)}) %all-reduce.39.cloned.1.call-update) | async-done | bytes 1048592 | tf_op jit(solution)/shard_map/psum | solution.py:38
  829.0 2.0 multiply_subtract_fusion.1
  831.0 1.0 copy-done.2
  832.0 9.1 convolution_bitcast_fusion.9
  841.2 36.0 %all-reduce.41.cloned.1.call-done = f32[2048,64]{1,0:T(8,128)} async-done(((f32[2048,64]{1,0:T(8,128)}), f32[2048,64]{1,0:T(8,128)}) %all-reduce.41.cloned.1.call-update) | async-done | bytes 524304 | tf_op jit(solution)/shard_map/psum | solution.py:36
  877.2 10.2 convolution_bitcast_fusion.1
  887.5 78.9 %all-reduce.43.cloned.1.call-done = f32[4096,64]{0,1:T(8,128)} async-done(((f32[4096,64]{0,1:T(8,128)}), f32[4096,64]{0,1:T(8,128)}) %all-reduce.43.cloned.1.call-update) | async-done | bytes 1048592 | tf_op jit(solution)/shard_map/psum | solution.py:38
  966.3 2.0 multiply_subtract_fusion
  968.4 1.0 copy-done.3
  969.4 9.1 convolution_bitcast_fusion.8
  978.8 35.7 %all-reduce.45.cloned.1.call-done = f32[2048,64]{1,0:T(8,128)} async-done(((f32[2048,64]{1,0:T(8,128)}), f32[2048,64]{1,0:T(8,128)}) %all-reduce.45.cloned.1.call-update) | async-done | bytes 524304 | tf_op jit(solution)/shard_map/psum | solution.py:36
  1014.6 10.3 convolution_bitcast_fusion
  1024.9 78.9 %all-reduce.47.cloned.1.call-done = f32[4096,64]{0,1:T(8,128)} async-done(((f32[4096,64]{0,1:T(8,128)}), f32[4096,64]{0,1:T(8,128)}) %all-reduce.47.cloned.1.call-update) | async-done | bytes 1048592 | tf_op jit(solution)/shard_map/psum | solution.py:38
  1103.8 2.6 multiply_reduce_fusion
  1106.4 5.7 stack.39
  1112.1 39.5 %psum.135 = f32[9]{0:T(128)S(1)} all-reduce(f32[9]{0:T(128)S(1)} %stack.39), channel_id=1, replica_groups=mesh['pair'=8,'aux'=4] {'pair','aux'}, use_global_device_ids=true, to_apply=%region_25.0 | all-reduce | flops 9 | bytes 72 | tf_op jit(solution)/shard_map/psum | solution.py:50
  1151.7 1.1 multiply_reduce_fusion.9
  (41 shorter events, 1.5 us)
Async XLA Ops:
  7.2 50.8 %copy-start.5 = (f32[2048]{0:T(1024)S(1)}, f32[2048]{0:T(1024)}, u32[]{:S(2)}) copy-start(f32[2048]{0:T(1024)} %param.5) | copy-start | bytes 24580
  7.2 50.8 %all-reduce.17.cloned.1.call-start = ((), (), s32[]{:S(2)}) async-start(), calls=%async_computation | async-start | bytes 2097152 | tf_op jit(solution)/shard_map/psum | solution.py:36
  18.8 128.5 %copy-start.4 = (f32[4096,64]{0,1:T(8,128)S(1)}, f32[4096,64]{0,1:T(8,128)}, u32[]{:S(2)}) copy-start(f32[4096,64]{0,1:T(8,128)} %param.6) | copy-start | bytes 3145732
  18.8 128.4 %all-reduce.19.cloned.1.call-start = ((), (), s32[]{:S(2)}) async-start(), calls=%async_computation.1 | async-start | bytes 2097152 | tf_op jit(solution)/shard_map/psum | solution.py:38
  68.3 125.5 %all-reduce.21.cloned.1.call-start = ((), (), s32[]{:S(2)}) async-start(), calls=%async_computation.2 | async-start | bytes 2097152 | tf_op jit(solution)/shard_map/psum | solution.py:36
  157.8 125.4 %all-reduce.23.cloned.1.call-start = ((), (), s32[]{:S(2)}) async-start(), calls=%async_computation.3 | async-start | bytes 2097152 | tf_op jit(solution)/shard_map/psum | solution.py:38
  204.1 125.7 %all-reduce.25.cloned.1.call-start = ((), (), s32[]{:S(2)}) async-start(), calls=%async_computation.4 | async-start | bytes 2097152 | tf_op jit(solution)/shard_map/psum | solution.py:36
  293.8 125.4 %all-reduce.27.cloned.1.call-start = ((), (), s32[]{:S(2)}) async-start(), calls=%async_computation.5 | async-start | bytes 2097152 | tf_op jit(solution)/shard_map/psum | solution.py:38
  340.1 125.7 %all-reduce.29.cloned.1.call-start = ((), (), s32[]{:S(2)}) async-start(), calls=%async_computation.6 | async-start | bytes 2097152 | tf_op jit(solution)/shard_map/psum | solution.py:36
  429.8 125.4 %all-reduce.31.cloned.1.call-start = ((), (), s32[]{:S(2)}) async-start(), calls=%async_computation.7 | async-start | bytes 2097152 | tf_op jit(solution)/shard_map/psum | solution.py:38
  476.1 126.6 %all-reduce.33.cloned.1.call-start = ((), (), s32[]{:S(2)}) async-start(), calls=%async_computation.8 | async-start | bytes 2097152 | tf_op jit(solution)/shard_map/psum | solution.py:36
  556.6 1.0 copy-start
  566.7 125.2 %all-reduce.35.cloned.1.call-start = ((), (), s32[]{:S(2)}) async-start(), calls=%async_computation.9 | async-start | bytes 2097152 | tf_op jit(solution)/shard_map/psum | solution.py:38
  613.0 126.8 %all-reduce.37.cloned.1.call-start = ((), (), s32[]{:S(2)}) async-start(), calls=%async_computation.10 | async-start | bytes 2097152 | tf_op jit(solution)/shard_map/psum | solution.py:36
  693.6 1.0 copy-start.1
  703.8 125.2 %all-reduce.39.cloned.1.call-start = ((), (), s32[]{:S(2)}) async-start(), calls=%async_computation.11 | async-start | bytes 2097152 | tf_op jit(solution)/shard_map/psum | solution.py:38
  750.1 127.0 %all-reduce.41.cloned.1.call-start = ((), (), s32[]{:S(2)}) async-start(), calls=%async_computation.12 | async-start | bytes 2097152 | tf_op jit(solution)/shard_map/psum | solution.py:36
  831.0 1.0 copy-start.2
  841.1 125.2 %all-reduce.43.cloned.1.call-start = ((), (), s32[]{:S(2)}) async-start(), calls=%async_computation.13 | async-start | bytes 2097152 | tf_op jit(solution)/shard_map/psum | solution.py:38
  887.4 127.1 %all-reduce.45.cloned.1.call-start = ((), (), s32[]{:S(2)}) async-start(), calls=%async_computation.14 | async-start | bytes 2097152 | tf_op jit(solution)/shard_map/psum | solution.py:36
  968.4 1.0 copy-start.3
  978.5 173.2 %copy-start.6 = (f32[9]{0:T(128)S(1)}, f32[9]{0:T(128)}, u32[]{:S(2)}) copy-start(f32[9]{0:T(128)} %constant.23.clone) | copy-start | bytes 112
  978.5 125.3 %all-reduce.47.cloned.1.call-start = ((), (), s32[]{:S(2)}) async-start(), calls=%async_computation.15 | async-start | bytes 2097152 | tf_op jit(solution)/shard_map/psum | solution.py:38
Sparse Core Ops, SparseCore 0:
  18.9 39.0 all-reduce.16
  68.4 78.7 all-reduce.18
  157.9 35.8 all-reduce.20
  204.3 78.8 all-reduce.22
  293.9 35.8 all-reduce.24
  340.3 78.8 all-reduce.26
  429.9 35.8 all-reduce.28
  476.2 78.8 all-reduce.30
  566.8 35.8 all-reduce.32
  613.1 78.7 all-reduce.34
  703.9 35.8 all-reduce.36
  750.2 78.7 all-reduce.38
  841.2 35.8 all-reduce.40
  887.5 78.7 all-reduce.42
  978.6 35.8 all-reduce.44
  1025.0 78.7 all-reduce.46
where the time goes:
time: 1170 us; the launch traced here: 1160 us
  waiting for transfers between devices  922 us (79%)
  matrix products  158 us (14%)
  blocking collectives  39.5 us (3%)
  other arithmetic  15.1 us (1%)
  between operations  14.3 us (1%)
    psum x8, waiting for transfers between devices, per_device(): lax.psum(lax.dot_general(pair_factors, scaled, (((0,), (0,)), ((), ())),...  631 us
    psum x8, waiting for transfers between devices, per_device(): rows = lax.psum(rows, 'aux')  290 us
    dot_general x8, matrix products, per_device(): lax.dot_general(pair_factors, scaled, (((0,), (0,)), ((), ())), preferred...  82.2 us
    dot_general x8, matrix products, per_device(): jnp.dot(pair_factors, current.astype(jnp.bfloat16), preferred_element_typ...  75.4 us
    psum x1, blocking collectives, per_device(): totals = lax.psum(jnp.stack(partials), ('pair', 'aux'))  39.5 us
  transfers between devices with their start and end apart: 16, of which 16 were waited for; matrix products, arithmetic and copies ran while one was open for 0% of the time, Pallas kernels for 0%

commit v1 on v0

--- a/solution.py
+++ b/solution.py
@@ -33,7 +33,9 @@
         rows = jnp.dot(
             pair_factors, current.astype(jnp.bfloat16), preferred_element_type=jnp.float32
         )
-        rows = lax.psum(rows, "aux")
+        rows = rows
+        for hop in (1, 2):
+            rows = rows + lax.ppermute(rows, "aux", [(dev, dev ^ hop) for dev in range(4)])
         scaled = (pair_weights[:, None] * rows).astype(jnp.bfloat16)
         image = lax.psum(
             lax.dot_general(

time: 1170 us -> 1010 us (0.86)
  waiting for transfers between devices: 922 us -> 740 us
  starting transfers between devices: 1.83 us -> 16.9 us
    psum x8 -> x0, waiting for transfers between devices: 290 us -> none  [per_device(): rows = lax.psum(rows, 'aux')]
    ppermute x0 -> x16, waiting for transfers between devices: none -> 116 us  [per_device(): lax.ppermute(rows, 'aux', [(dev, dev ^ hop) for dev in range(4)])]
    dot_general x8, matrix products: 75.4 us -> 93.3 us  [per_device(): jnp.dot(pair_factors, current.astype(jnp.bfloat16), preferred_element_typ...]
    ppermute x0 -> x16, starting transfers between devices: none -> 14.3 us  [per_device(): lax.ppermute(rows, 'aux', [(dev, dev ^ hop) for dev in range(4)])]
  transfers between devices with their start and end apart: 16 -> 24, of which waited for: 16 -> 24; matrix products, arithmetic and copies ran while one was open for 0% -> 0% of each run, Pallas kernels for 0% -> 0%
where the time goes in v1:
time: 1010 us
  waiting for transfers between devices  740 us (73%)
  matrix products  166 us (16%)
  blocking collectives  39.5 us (4%)
  other arithmetic  24.9 us (2%)
  starting transfers between devices  16.9 us (2%)
  between operations  14.4 us (1%)
    psum x8, waiting for transfers between devices, per_device(): lax.psum(lax.dot_general(pair_factors, scaled, (((0,), (0,)), ((), ())),...  624 us
    ppermute x16, waiting for transfers between devices, per_device(): lax.ppermute(rows, 'aux', [(dev, dev ^ hop) for dev in range(4)])  116 us
    dot_general x8, matrix products, per_device(): jnp.dot(pair_factors, current.astype(jnp.bfloat16), preferred_element_typ...  93.3 us
    dot_general x8, matrix products, per_device(): lax.dot_general(pair_factors, scaled, (((0,), (0,)), ((), ())), preferred...  72.9 us
    psum x1, blocking collectives, per_device(): totals = lax.psum(jnp.stack(partials), ('pair', 'aux'))  39.5 us
  transfers between devices with their start and end apart: 24, of which 24 were waited for; matrix products, arithmetic and copies ran while one was open for 0% of the time, Pallas kernels for 0%

profile of v1, /device:TPU:0, one launch (start us, length us, event | category | flops | bytes accessed | tf_op | source)
XLA Modules:
  0.0 1007.4 jit_solution(15265576410393871616)
XLA Ops:
  7.2 11.3 %fusion.7 = f32[2048,64]{0,1:T(8,128)S(1)} fusion(bf16[2048,4096]{1,0:T(8,128)(2,1)} %param.4, f32[4096,64]{0,1:T(8,128)} %param.6), kind=kOutput, calls=%fused_computation.37 | convolution fusion | flops 1074003968 | bytes 18350080 | tf_op jit(solution)/shard_map/dot_general | solution.py:33
  19.1 1.5 collective-permute-done
  20.7 2.9 collective-permute-start.1
  23.6 12.2 %collective-permute-done.1 = f32[2048,64]{0,1:T(8,128)S(1)} collective-permute-done((f32[2048,64]{0,1:T(8,128)S(1)}, f32[2048,64]{0,1:T(8,128)S(1)}, u32[]{:S(2)}, u32[]{:S(2)}) %collective-permute-start.1) | collective-permute-done | bytes 524320 | tf_op jit(solution)/shard_map/ppermute | solution.py:38
  35.9 4.1 convolution_bitcast_fusion.7
  40.6 79.4 %all-reduce.9.cloned.1.call-done = f32[4096,64]{0,1:T(8,128)} async-done(((f32[4096,64]{0,1:T(8,128)}), f32[4096,64]{0,1:T(8,128)}) %all-reduce.9.cloned.1.call-update) | async-done | bytes 1048592 | tf_op jit(solution)/shard_map/psum | solution.py:40
  121.4 11.0 %convolution_bitcast_fusion.14 = f32[2048,64]{0,1:T(8,128)S(1)} fusion(bf16[2048,4096]{1,0:T(8,128)(2,1)} %param.4, f32[4096,64]{0,1:T(8,128)S(1)} %multiply_subtract_fusion.6), kind=kOutput, calls=%fused_computation.14 | convolution fusion | flops 1074003968 | bytes 18350080 | tf_op jit(solution)/shard_map/dot_general | solution.py:33
  132.4 1.9 collective-permute-done.2
  135.9 12.5 %collective-permute-done.3 = f32[2048,64]{0,1:T(8,128)S(1)} collective-permute-done((f32[2048,64]{0,1:T(8,128)S(1)}, f32[2048,64]{0,1:T(8,128)S(1)}, u32[]{:S(2)}, u32[]{:S(2)}) %collective-permute-start.3) | collective-permute-done | bytes 524320 | tf_op jit(solution)/shard_map/ppermute | solution.py:38
  148.4 9.8 convolution_bitcast_fusion.6
  158.5 77.9 %all-reduce.11.cloned.1.call-done = f32[4096,64]{0,1:T(8,128)} async-done(((f32[4096,64]{0,1:T(8,128)}), f32[4096,64]{0,1:T(8,128)}) %all-reduce.11.cloned.1.call-update) | async-done | bytes 1048592 | tf_op jit(solution)/shard_map/psum | solution.py:40
  237.8 11.0 %convolution_bitcast_fusion.13 = f32[2048,64]{0,1:T(8,128)S(1)} fusion(bf16[2048,4096]{1,0:T(8,128)(2,1)} %param.4, f32[4096,64]{0,1:T(8,128)S(1)} %multiply_subtract_fusion.5), kind=kOutput, calls=%fused_computation.13 | convolution fusion | flops 1074003968 | bytes 18350080 | tf_op jit(solution)/shard_map/dot_general | solution.py:33
  248.8 1.9 collective-permute-done.4
  252.3 12.5 %collective-permute-done.5 = f32[2048,64]{0,1:T(8,128)S(1)} collective-permute-done((f32[2048,64]{0,1:T(8,128)S(1)}, f32[2048,64]{0,1:T(8,128)S(1)}, u32[]{:S(2)}, u32[]{:S(2)}) %collective-permute-start.5) | collective-permute-done | bytes 524320 | tf_op jit(solution)/shard_map/ppermute | solution.py:38
  264.8 9.8 convolution_bitcast_fusion.5
  275.0 77.8 %all-reduce.13.cloned.1.call-done = f32[4096,64]{0,1:T(8,128)} async-done(((f32[4096,64]{0,1:T(8,128)}), f32[4096,64]{0,1:T(8,128)}) %all-reduce.13.cloned.1.call-update) | async-done | bytes 1048592 | tf_op jit(solution)/shard_map/psum | solution.py:40
  354.2 11.7 %convolution_bitcast_fusion.12 = f32[2048,64]{0,1:T(8,128)} fusion(bf16[2048,4096]{1,0:T(8,128)(2,1)} %param.4, f32[4096,64]{0,1:T(8,128)S(1)} %multiply_subtract_fusion.4), kind=kOutput, calls=%fused_computation.12 | convolution fusion | flops 1074003968 | bytes 18350080 | tf_op jit(solution)/shard_map/dot_general | solution.py:33
  365.9 2.1 collective-permute-done.6
  370.7 12.5 %collective-permute-done.7 = f32[2048,64]{0,1:T(8,128)S(1)} collective-permute-done((f32[2048,64]{0,1:T(8,128)S(1)}, f32[2048,64]{0,1:T(8,128)S(1)}, u32[]{:S(2)}, u32[]{:S(2)}) %collective-permute-start.7) | collective-permute-done | bytes 524320 | tf_op jit(solution)/shard_map/ppermute | solution.py:38
  383.2 9.8 convolution_bitcast_fusion.4
  393.3 77.8 %all-reduce.15.cloned.1.call-done = f32[4096,64]{0,1:T(8,128)} async-done(((f32[4096,64]{0,1:T(8,128)}), f32[4096,64]{0,1:T(8,128)}) %all-reduce.15.cloned.1.call-update) | async-done | bytes 1048592 | tf_op jit(solution)/shard_map/psum | solution.py:40
  471.1 2.4 multiply_subtract_fusion.3
  473.5 12.1 %convolution_bitcast_fusion.11 = f32[2048,64]{0,1:T(8,128)} fusion(bf16[2048,4096]{1,0:T(8,128)(2,1)} %param.4, f32[4096,64]{0,1:T(8,128)} %multiply_subtract_fusion.3), kind=kOutput, calls=%fused_computation.11 | convolution fusion | flops 1074003968 | bytes 18350080 | tf_op jit(solution)/shard_map/dot_general | solution.py:33
  485.6 2.1 collective-permute-done.8
  490.4 12.5 %collective-permute-done.9 = f32[2048,64]{0,1:T(8,128)S(1)} collective-permute-done((f32[2048,64]{0,1:T(8,128)S(1)}, f32[2048,64]{0,1:T(8,128)S(1)}, u32[]{:S(2)}, u32[]{:S(2)}) %collective-permute-start.9) | collective-permute-done | bytes 524320 | tf_op jit(solution)/shard_map/ppermute | solution.py:38
  502.9 9.9 convolution_bitcast_fusion.3
  513.1 77.7 %all-reduce.17.cloned.1.call-done = f32[4096,64]{0,1:T(8,128)} async-done(((f32[4096,64]{0,1:T(8,128)}), f32[4096,64]{0,1:T(8,128)}) %all-reduce.17.cloned.1.call-update) | async-done | bytes 1048592 | tf_op jit(solution)/shard_map/psum | solution.py:40
  590.8 2.8 multiply_subtract_fusion.2
  593.6 12.1 %convolution_bitcast_fusion.10 = f32[2048,64]{0,1:T(8,128)} fusion(bf16[2048,4096]{1,0:T(8,128)(2,1)} %param.4, f32[4096,64]{0,1:T(8,128)} %multiply_subtract_fusion.2), kind=kOutput, calls=%fused_computation.10 | convolution fusion | flops 1074003968 | bytes 18350080 | tf_op jit(solution)/shard_map/dot_general | solution.py:33
  605.6 2.1 collective-permute-done.10
  610.4 12.5 %collective-permute-done.11 = f32[2048,64]{0,1:T(8,128)S(1)} collective-permute-done((f32[2048,64]{0,1:T(8,128)S(1)}, f32[2048,64]{0,1:T(8,128)S(1)}, u32[]{:S(2)}, u32[]{:S(2)}) %collective-permute-start.11) | collective-permute-done | bytes 524320 | tf_op jit(solution)/shard_map/ppermute | solution.py:38
  622.9 9.8 convolution_bitcast_fusion.2
  633.3 77.5 %all-reduce.19.cloned.1.call-done = f32[4096,64]{0,1:T(8,128)} async-done(((f32[4096,64]{0,1:T(8,128)}), f32[4096,64]{0,1:T(8,128)}) %all-reduce.19.cloned.1.call-update) | async-done | bytes 1048592 | tf_op jit(solution)/shard_map/psum | solution.py:40
  710.8 3.0 multiply_subtract_fusion.1
  713.8 12.1 %convolution_bitcast_fusion.9 = f32[2048,64]{0,1:T(8,128)} fusion(bf16[2048,4096]{1,0:T(8,128)(2,1)} %param.4, f32[4096,64]{0,1:T(8,128)} %multiply_subtract_fusion.1), kind=kOutput, calls=%fused_computation.9 | convolution fusion | flops 1074003968 | bytes 18350080 | tf_op jit(solution)/shard_map/dot_general | solution.py:33
  725.9 2.1 collective-permute-done.12
  730.7 12.5 %collective-permute-done.13 = f32[2048,64]{0,1:T(8,128)S(1)} collective-permute-done((f32[2048,64]{0,1:T(8,128)S(1)}, f32[2048,64]{0,1:T(8,128)S(1)}, u32[]{:S(2)}, u32[]{:S(2)}) %collective-permute-start.13) | collective-permute-done | bytes 524320 | tf_op jit(solution)/shard_map/ppermute | solution.py:38
  743.2 9.8 convolution_bitcast_fusion.1
  753.3 77.9 %all-reduce.21.cloned.1.call-done = f32[4096,64]{0,1:T(8,128)} async-done(((f32[4096,64]{0,1:T(8,128)}), f32[4096,64]{0,1:T(8,128)}) %all-reduce.21.cloned.1.call-update) | async-done | bytes 1048592 | tf_op jit(solution)/shard_map/psum | solution.py:40
  831.1 3.0 multiply_subtract_fusion
  834.1 12.1 %convolution_bitcast_fusion.8 = f32[2048,64]{0,1:T(8,128)} fusion(bf16[2048,4096]{1,0:T(8,128)(2,1)} %param.4, f32[4096,64]{0,1:T(8,128)} %multiply_subtract_fusion), kind=kOutput, calls=%fused_computation.8 | convolution fusion | flops 1074003968 | bytes 18350080 | tf_op jit(solution)/shard_map/dot_general | solution.py:33
  846.2 2.1 collective-permute-done.14
  851.0 12.5 %collective-permute-done.15 = f32[2048,64]{0,1:T(8,128)S(1)} collective-permute-done((f32[2048,64]{0,1:T(8,128)S(1)}, f32[2048,64]{0,1:T(8,128)S(1)}, u32[]{:S(2)}, u32[]{:S(2)}) %collective-permute-start.15) | collective-permute-done | bytes 524320 | tf_op jit(solution)/shard_map/ppermute | solution.py:38
  863.5 9.8 convolution_bitcast_fusion
  873.4 78.0 %all-reduce.23.cloned.1.call-done = f32[4096,64]{0,1:T(8,128)} async-done(((f32[4096,64]{0,1:T(8,128)}), f32[4096,64]{0,1:T(8,128)}) %all-reduce.23.cloned.1.call-update) | async-done | bytes 1048592 | tf_op jit(solution)/shard_map/psum | solution.py:40
  951.4 2.6 multiply_reduce_fusion
  954.0 5.7 stack.39
  959.7 39.5 %psum.71 = f32[9]{0:T(128)S(1)} all-reduce(f32[9]{0:T(128)S(1)} %stack.39), channel_id=1, replica_groups=mesh['pair'=8,'aux'=4] {'pair','aux'}, use_global_device_ids=true, to_apply=%region_17.0 | all-reduce | flops 9 | bytes 72 | tf_op jit(solution)/shard_map/psum | solution.py:52
  (51 shorter events, 25.2 us)
Async XLA Ops:
  7.2 28.7 %copy-start.2 = (f32[2048]{0:T(1024)S(1)}, f32[2048]{0:T(1024)}, u32[]{:S(2)}) copy-start(f32[2048]{0:T(1024)} %param.5) | copy-start | bytes 24580
  7.2 112.9 %all-reduce.9.cloned.1.call-start = ((), (), s32[]{:S(2)}) async-start(), calls=%async_computation | async-start | bytes 2097152 | tf_op jit(solution)/shard_map/psum | solution.py:40
  7.2 28.6 %copy-start = (bf16[2048,4096]{1,0:T(8,128)(2,1)S(1)}, bf16[2048,4096]{1,0:T(8,128)(2,1)}, u32[]{:S(2)}) copy-start(bf16[2048,4096]{1,0:T(8,128)(2,1)} %param.4) | copy-start | bytes 50331652
  18.6 101.5 %copy-start.1 = (f32[4096,64]{0,1:T(8,128)S(1)}, f32[4096,64]{0,1:T(8,128)}, u32[]{:S(2)}) copy-start(f32[4096,64]{0,1:T(8,128)} %param.6) | copy-start | bytes 3145732
  18.6 2.1 collective-permute-start
  20.7 15.1 %collective-permute-start.1 = (f32[2048,64]{0,1:T(8,128)S(1)}, f32[2048,64]{0,1:T(8,128)S(1)}, u32[]{:S(2)}, u32[]{:S(2)}) collective-permute-start(f32[2048,64]{0,1:T(8,128)S(1)} %add.78), channel_id=1, source_target_pairs={{0,2},{1,3},{2,0},{3,1},{4,6},{5,7},{6,4},{7,5},{8,10},{9,11},{10,... | collective-permute-start | bytes 1572872 | tf_op jit(solution)/shard_map/ppermute | solution.py:38
  40.0 196.4 %all-reduce.11.cloned.1.call-start = ((), (), s32[]{:S(2)}) async-start(), calls=%async_computation.1 | async-start | bytes 2097152 | tf_op jit(solution)/shard_map/psum | solution.py:40
  132.4 2.0 collective-permute-start.2
  134.4 14.0 %collective-permute-start.3 = (f32[2048,64]{0,1:T(8,128)S(1)}, f32[2048,64]{0,1:T(8,128)S(1)}, u32[]{:S(2)}, u32[]{:S(2)}) collective-permute-start(f32[2048,64]{0,1:T(8,128)S(1)} %add.80), channel_id=1, source_target_pairs={{0,2},{1,3},{2,0},{3,1},{4,6},{5,7},{6,4},{7,5},{8,10},{9,11},{10,... | collective-permute-start | bytes 1572872 | tf_op jit(solution)/shard_map/ppermute | solution.py:38
  158.3 194.5 %all-reduce.13.cloned.1.call-start = ((), (), s32[]{:S(2)}) async-start(), calls=%async_computation.2 | async-start | bytes 2097152 | tf_op jit(solution)/shard_map/psum | solution.py:40
  248.8 2.0 collective-permute-start.4
  250.8 14.0 %collective-permute-start.5 = (f32[2048,64]{0,1:T(8,128)S(1)}, f32[2048,64]{0,1:T(8,128)S(1)}, u32[]{:S(2)}, u32[]{:S(2)}) collective-permute-start(f32[2048,64]{0,1:T(8,128)S(1)} %add.82), channel_id=1, source_target_pairs={{0,2},{1,3},{2,0},{3,1},{4,6},{5,7},{6,4},{7,5},{8,10},{9,11},{10,... | collective-permute-start | bytes 1572872 | tf_op jit(solution)/shard_map/ppermute | solution.py:38
  274.7 196.4 %all-reduce.15.cloned.1.call-start = ((), (), s32[]{:S(2)}) async-start(), calls=%async_computation.3 | async-start | bytes 2097152 | tf_op jit(solution)/shard_map/psum | solution.py:40
  365.9 2.1 collective-permute-start.6
  369.1 14.0 %collective-permute-start.7 = (f32[2048,64]{0,1:T(8,128)S(1)}, f32[2048,64]{0,1:T(8,128)S(1)}, u32[]{:S(2)}, u32[]{:S(2)}) collective-permute-start(f32[2048,64]{0,1:T(8,128)S(1)} %add.84), channel_id=1, source_target_pairs={{0,2},{1,3},{2,0},{3,1},{4,6},{5,7},{6,4},{7,5},{8,10},{9,11},{10,... | collective-permute-start | bytes 1572872 | tf_op jit(solution)/shard_map/ppermute | solution.py:38
  393.0 197.8 %all-reduce.17.cloned.1.call-start = ((), (), s32[]{:S(2)}) async-start(), calls=%async_computation.4 | async-start | bytes 2097152 | tf_op jit(solution)/shard_map/psum | solution.py:40
  485.6 2.1 collective-permute-start.8
  488.9 14.0 %collective-permute-start.9 = (f32[2048,64]{0,1:T(8,128)S(1)}, f32[2048,64]{0,1:T(8,128)S(1)}, u32[]{:S(2)}, u32[]{:S(2)}) collective-permute-start(f32[2048,64]{0,1:T(8,128)S(1)} %add.86), channel_id=1, source_target_pairs={{0,2},{1,3},{2,0},{3,1},{4,6},{5,7},{6,4},{7,5},{8,10},{9,11},{10,... | collective-permute-start | bytes 1572872 | tf_op jit(solution)/shard_map/ppermute | solution.py:38
  512.8 198.0 %all-reduce.19.cloned.1.call-start = ((), (), s32[]{:S(2)}) async-start(), calls=%async_computation.5 | async-start | bytes 2097152 | tf_op jit(solution)/shard_map/psum | solution.py:40
  605.6 2.1 collective-permute-start.10
  608.9 14.0 %collective-permute-start.11 = (f32[2048,64]{0,1:T(8,128)S(1)}, f32[2048,64]{0,1:T(8,128)S(1)}, u32[]{:S(2)}, u32[]{:S(2)}) collective-permute-start(f32[2048,64]{0,1:T(8,128)S(1)} %add.88), channel_id=1, source_target_pairs={{0,2},{1,3},{2,0},{3,1},{4,6},{5,7},{6,4},{7,5},{8,10},{9,11},{10,... | collective-permute-start | bytes 1572872 | tf_op jit(solution)/shard_map/ppermute | solution.py:38
  632.8 198.4 %all-reduce.21.cloned.1.call-start = ((), (), s32[]{:S(2)}) async-start(), calls=%async_computation.6 | async-start | bytes 2097152 | tf_op jit(solution)/shard_map/psum | solution.py:40
  725.9 2.1 collective-permute-start.12
  729.2 14.0 %collective-permute-start.13 = (f32[2048,64]{0,1:T(8,128)S(1)}, f32[2048,64]{0,1:T(8,128)S(1)}, u32[]{:S(2)}, u32[]{:S(2)}) collective-permute-start(f32[2048,64]{0,1:T(8,128)S(1)} %add.90), channel_id=1, source_target_pairs={{0,2},{1,3},{2,0},{3,1},{4,6},{5,7},{6,4},{7,5},{8,10},{9,11},{10,... | collective-permute-start | bytes 1572872 | tf_op jit(solution)/shard_map/ppermute | solution.py:38
  753.0 198.3 %all-reduce.23.cloned.1.call-start = ((), (), s32[]{:S(2)}) async-start(), calls=%async_computation.7 | async-start | bytes 2097152 | tf_op jit(solution)/shard_map/psum | solution.py:40
  846.2 153.0 %copy-start.3 = (f32[9]{0:T(128)S(1)}, f32[9]{0:T(128)}, u32[]{:S(2)}) copy-start(f32[9]{0:T(128)} %constant.23.clone) | copy-start | bytes 112
  846.2 2.1 collective-permute-start.14
  849.5 14.0 %collective-permute-start.15 = (f32[2048,64]{0,1:T(8,128)S(1)}, f32[2048,64]{0,1:T(8,128)S(1)}, u32[]{:S(2)}, u32[]{:S(2)}) collective-permute-start(f32[2048,64]{0,1:T(8,128)S(1)} %add.92), channel_id=1, source_target_pairs={{0,2},{1,3},{2,0},{3,1},{4,6},{5,7},{6,4},{7,5},{8,10},{9,11},{10,... | collective-permute-start | bytes 1572872 | tf_op jit(solution)/shard_map/ppermute | solution.py:38
Sparse Core Ops, SparseCore 0:
  40.1 79.8 all-reduce.8
  158.4 77.9 all-reduce.10
  274.8 77.8 all-reduce.12
  393.1 77.9 all-reduce.14
  512.9 77.8 all-reduce.16
  632.9 77.9 all-reduce.18
  753.2 77.9 all-reduce.20
  873.5 77.8 all-reduce.22
